TPU v7x, 512 devices: a whole 4x4x16 slice. The times are simulated.
512 devices in a mesh: rep: 64 (over x_lo, z, core), tp: 8 (over y, x_hi).
Axes of the slice: x: 4 (x_hi: 2, x_lo: 2; x = x_hi * 2 + x_lo), y: 4, z: 16, core: 2. Of those that a mesh axis runs over, the one named last changes fastest.
Arguments:
- prompt_q: bfloat16 [32768, 2048], P('rep', 'tp'), may hold values from -24 to 24
- prompt_k: bfloat16 [32768, 2048], P('rep', 'tp'), may hold values from -24 to 24
- prompt_v: bfloat16 [32768, 2048], P('rep', 'tp'), may hold values from -6 to 6
- prompt_len: int32 [64], P('rep'), may hold values from 256 to 512, as said below
- cache_keys: bfloat16 [128, 1024, 2048], P('rep', None, 'tp'), may hold values from -24 to 24
- cache_values: bfloat16 [128, 1024, 2048], P('rep', None, 'tp'), may hold values from -6 to 6
- new_q: bfloat16 [128, 2048], P('rep', 'tp'), may hold values from -24 to 24
- new_k: bfloat16 [128, 2048], P('rep', 'tp'), may hold values from -6 to 6
- new_v: bfloat16 [128, 2048], P('rep', 'tp'), may hold values from -6 to 6
- cache_len: int32 [128], replicated, may hold values from 260 to 1024, as said below
- moving: int32 [64], replicated, may hold values from 0 to 1
- out_weight: bfloat16 [2048, 2048], P(None, 'tp'), may hold values from -0.125 to 0.125
- out_bias: float32 [2048], P('tp'), may hold values from -1.75 to 1.75
- residual: bfloat16 [32896, 2048], P('rep', 'tp'), may hold values from -150 to 150
- ln_gain: float32 [2048], P('tp'), may hold values from 0.1 to 1.9
- ln_shift: float32 [2048], P('tp'), may hold values from -1.75 to 1.75
Outputs:
- hidden_out: bfloat16 [32896, 2048], P('rep', 'tp')
- normed: bfloat16 [32896, 2048], P('rep', 'tp')
- moved_window: bfloat16 [64, 2, 260, 2048], P('rep', None, None, 'tp')
Inputs may be any that keep to these rules, and one draw needn't show every extreme that they name: `prompt_len`: some replica's prompt has all 512 tokens live. `cache_len`: some request's cache is full.
All inputs are finite; a program needn't handle non-finite values.
Results may differ from a plain program's by a relative error of at most 0.0022.
Values may be sent and summed in bfloat16 or wider, within the bound.
No kernel may reach another device: no remote copies, remote signals or barrier semaphores. Data moves between devices by JAX's collectives and lax.ppermute only.
A program may use at most 64 MiB of HBM per device.

v0:
```python
import math
import jax
import jax.numpy as jnp
from jax import lax
from jax.sharding import PartitionSpec as P

D = 2048
HEADS = 16
HD = 128
SINK = 4
WIN = 256
masked_score = -1e30
norm_epsilon = 1e-05


def from_behind(block, axis, distance):
    devices = range(lax.axis_size(axis))
    route = [((i - distance) % len(devices), i) for i in devices]
    return lax.ppermute(block, axis, route)


def head_slopes(local_heads):
    first_head = lax.axis_index("tp") * local_heads
    head_ids = (first_head + jnp.arange(local_heads, dtype=jnp.int32)).astype(jnp.float32)
    return jnp.exp2(-8.0 * (head_ids + 1.0) / HEADS)


def softmax_rows(scores):
    row_max = jnp.max(scores, axis=-1, keepdims=True)
    expo_terms = jnp.exp(scores - row_max)
    return (expo_terms / jnp.sum(expo_terms, axis=-1, keepdims=True)).astype(jnp.bfloat16)


def prompt_attend(query_rows, key_rows, value_rows, length, slopes):
    row_count = query_rows.shape[0]
    local_heads = slopes.shape[0]
    query_heads = query_rows.reshape(row_count, local_heads, HD)
    key_heads = key_rows.reshape(row_count, local_heads, HD)
    value_heads = value_rows.reshape(row_count, local_heads, HD)
    scores = jnp.einsum(
        "qhd,khd->hqk", query_heads, key_heads, preferred_element_type=jnp.float32
    ) * (1.0 / math.sqrt(HD))
    position = jnp.arange(row_count, dtype=jnp.int32)
    distance = (position[:, None] - position[None, :]).astype(jnp.float32)
    scores = scores - slopes[:, None, None] * distance[None]
    allowed = (position[None, :] <= position[:, None]) & (position[None, :] < length)
    scores = jnp.where(allowed[None], scores, masked_score)
    weights = softmax_rows(scores)
    mixed_heads = jnp.einsum(
        "hqk,khd->qhd", weights, value_heads, preferred_element_type=jnp.float32
    )
    return mixed_heads.astype(jnp.bfloat16).reshape(row_count, local_heads * HD)


def window_rows(cache_rows, newest, length):
    middle = lax.dynamic_slice_in_dim(cache_rows, length + 1 - WIN, WIN - 1, 0)
    return jnp.concatenate([cache_rows[:SINK], middle, newest[None]], axis=0)


def window_positions(length):
    sink_part = jnp.arange(SINK, dtype=jnp.int32)
    tail_part = length + 1 - WIN + jnp.arange(WIN, dtype=jnp.int32)
    return jnp.concatenate([sink_part, tail_part])


def decode_attend(query_row, key_window, value_window, length, slopes):
    local_heads = slopes.shape[0]
    query_heads = query_row.reshape(local_heads, HD)
    key_heads = key_window.reshape(-1, local_heads, HD)
    value_heads = value_window.reshape(-1, local_heads, HD)
    scores = jnp.einsum(
        "hd,whd->hw", query_heads, key_heads, preferred_element_type=jnp.float32
    ) * (1.0 / math.sqrt(HD))
    distance = (length - window_positions(length)).astype(jnp.float32)
    scores = scores - slopes[:, None] * distance[None, :]
    weights = softmax_rows(scores)
    mixed_heads = jnp.einsum("hw,whd->hd", weights, value_heads, preferred_element_type=jnp.float32)
    return mixed_heads.astype(jnp.bfloat16).reshape(local_heads * HD)


def select_slot(stacked, slot_index):
    return lax.dynamic_index_in_dim(stacked, slot_index, 0, keepdims=False)


def on_device(
    prompt_q,
    prompt_k,
    prompt_v,
    prompt_len,
    cache_keys,
    cache_values,
    new_q,
    new_k,
    new_v,
    cache_len,
    moving,
    out_weight,
    out_bias,
    residual,
    ln_gain,
    ln_shift,
):
    replica_count = lax.axis_size("rep")
    replica_index = lax.axis_index("rep")
    partner = (replica_index + replica_count // 2) % replica_count
    local_heads = prompt_q.shape[1] // HD
    slopes = head_slopes(local_heads)
    prompt_mix = prompt_attend(prompt_q, prompt_k, prompt_v, prompt_len[0], slopes)
    slot_count = cache_keys.shape[0]
    leaving = moving[replica_index]
    staying = 1 - leaving
    stay_len = cache_len[replica_index * slot_count + staying]
    come_len = cache_len[partner * slot_count + moving[partner]]
    stay_keys = window_rows(select_slot(cache_keys, staying), select_slot(new_k, staying), stay_len)
    stay_values = window_rows(
        select_slot(cache_values, staying), select_slot(new_v, staying), stay_len
    )
    stay_out = decode_attend(select_slot(new_q, staying), stay_keys, stay_values, stay_len, slopes)
    come_cache_keys, come_cache_values, come_query, come_key, come_value = from_behind(
        (
            select_slot(cache_keys, leaving),
            select_slot(cache_values, leaving),
            select_slot(new_q, leaving),
            select_slot(new_k, leaving),
            select_slot(new_v, leaving),
        ),
        "rep",
        replica_count // 2,
    )
    come_keys = window_rows(come_cache_keys, come_key, come_len)
    come_values = window_rows(come_cache_values, come_value, come_len)
    come_out = decode_attend(come_query, come_keys, come_values, come_len, slopes)
    mixed_rows = jnp.concatenate([prompt_mix, stay_out[None], come_out[None]], axis=0)
    projected = jnp.dot(
        lax.all_gather(mixed_rows, "tp", axis=1, tiled=True),
        out_weight,
        preferred_element_type=jnp.float32,
    )
    stream = projected + out_bias[None, :] + residual.astype(jnp.float32)
    hidden_out = stream.astype(jnp.bfloat16)
    row_total = jnp.sum(stream, axis=1)
    row_mean = lax.psum(row_total, "tp") / D
    centered = stream - row_mean[:, None]
    row_var = lax.psum(jnp.sum(centered * centered, axis=1), "tp") / D
    normed = (
        centered * lax.rsqrt(row_var + norm_epsilon)[:, None] * ln_gain[None, :] + ln_shift[None, :]
    ).astype(jnp.bfloat16)
    moved_window = jnp.stack([come_keys, come_values], axis=0)[None]
    return (hidden_out, normed, moved_window)


def solution(mesh):
    in_specs = (
        P("rep", "tp"),
        P("rep", "tp"),
        P("rep", "tp"),
        P("rep"),
        P("rep", None, "tp"),
        P("rep", None, "tp"),
        P("rep", "tp"),
        P("rep", "tp"),
        P("rep", "tp"),
        P(),
        P(),
        P(None, "tp"),
        P("tp"),
        P("rep", "tp"),
        P("tp"),
        P("tp"),
    )
    out_specs = (P("rep", "tp"), P("rep", "tp"), P("rep", None, None, "tp"))
    return jax.shard_map(
        on_device, mesh=mesh, in_specs=in_specs, out_specs=out_specs, check_vma=False
    )
```

profile of v0, /device:TPU:32, one launch (start us, length us, event | category | flops | bytes accessed | tf_op | source)
XLA Modules:
  0.0 192.9 jit_solution(14140378695549050792)
XLA Ops:
  7.3 1.3 fusion.47
  10.6 1.1 dynamic-slice_bitcast_fusion.1
  11.6 3.4 %collective-permute-start.1 = (bf16[1024,256]{1,0:T(8,128)(2,1)S(1)}, bf16[1024,256]{1,0:T(8,128)(2,1)}, u32[]{:S(2)}, u32[]{:S(2)}) collective-permute-start(bf16[1024,256]{1,0:T(8,128)(2,1)S(1)} %dynamic-slice_bitcast_fusion.1), channel_id=1, source_target_pairs={{256,0},{264,8},{272,16},{280,24},{288,32},{296,40},{304,48},{312,... | collective-permute-start | bytes 1572872 | tf_op jit(solution)/shard_map/ppermute | solution.py:19
  16.3 1.4 fusion.33
  17.7 2.4 %collective-permute-start.2 = (bf16[256]{0:T(256)(128)(2,1)}, bf16[256]{0:T(256)(128)(2,1)}, u32[]{:S(2)}, u32[]{:S(2)}) collective-permute-start(bf16[256]{0:T(256)(128)(2,1)} %get-tuple-element.10), channel_id=1, source_target_pairs={{256,0},{264,8},{272,16},{280,24},{288,32},{296,40},{304,48},{312,... | collective-permute-start | bytes 1544 | tf_op jit(solution)/shard_map/ppermute | solution.py:19
  20.2 1.2 fusion.35
  21.4 3.4 %collective-permute-start = (bf16[256]{0:T(256)(128)(2,1)}, bf16[256]{0:T(256)(128)(2,1)}, u32[]{:S(2)}, u32[]{:S(2)}) collective-permute-start(bf16[256]{0:T(256)(128)(2,1)} %fusion.35), channel_id=1, source_target_pairs={{256,0},{264,8},{272,16},{280,24},{288,32},{296,40},{304,48},{312,... | collective-permute-start | bytes 1544 | tf_op jit(solution)/shard_map/ppermute | solution.py:19
  24.8 1.1 dynamic-slice_bitcast_fusion
  25.9 2.4 %collective-permute-start.3 = (bf16[1024,256]{1,0:T(8,128)(2,1)S(1)}, bf16[1024,256]{1,0:T(8,128)(2,1)}, u32[]{:S(2)}, u32[]{:S(2)}) collective-permute-start(bf16[1024,256]{1,0:T(8,128)(2,1)S(1)} %dynamic-slice_bitcast_fusion), channel_id=1, source_target_pairs={{256,0},{264,8},{272,16},{280,24},{288,32},{296,40},{304,48},{312,... | collective-permute-start | bytes 1572872 | tf_op jit(solution)/shard_map/ppermute | solution.py:19
  28.9 3.4 %collective-permute-start.4 = (bf16[256]{0:T(256)(128)(2,1)}, bf16[256]{0:T(256)(128)(2,1)}, u32[]{:S(2)}, u32[]{:S(2)}) collective-permute-start(bf16[256]{0:T(256)(128)(2,1)} %get-tuple-element.12), channel_id=1, source_target_pairs={{256,0},{264,8},{272,16},{280,24},{288,32},{296,40},{304,48},{312,... | collective-permute-start | bytes 1544 | tf_op jit(solution)/shard_map/ppermute | solution.py:19
  38.1 1.0 constant_dynamic-slice_fusion.6
  41.2 1.8 copy.50
  43.0 2.0 %fusion.24 = (f32[260]{0:T(512)S(1)}, f32[260]{0:T(512)S(1)}) fusion(s32[4]{0:T(128)S(1)} %iota.55, s32[256]{0:T(256)} %get-tuple-element.30, s32[]{:T(128)} %bitcast.6, s32[256]{0:T(256)} %get-tuple-element.29, s32[]{:T(128)} %bitcast.15), kind=kLoop, calls=%fused_computation.60 | loop fusion | flops 1560 | bytes 4152 | tf_op jit(solution)/shard_map/convert_element_type | solution.py:74
  45.0 1.5 pad_maximum_fusion.2
  46.5 3.0 %subtract_select_fusion = f32[2,512,512]{1,2,0:T(8,128)} fusion(f32[512,512]{0,1:T(8,128)S(1)} %subtract_convert_fusion, f32[2]{0:T(128)} %multiply_exponential_fusion, pred[512,512]{0,1:T(8,128)(4,1)S(1)} %fusion.2, bf16[512,256]{1,0:T(8,128)(2,1)} %param.17, bf16[512,256]{1,0:T(8,128)(2,1)} %param.16), kind=kOutput, calls=%fused_computation.3 | convolution fusion | flops 136314880 | bytes 3932168 | tf_op jit(solution)/shard_map/qhd,khd->hqk/dot_general | solution.py:40
  49.5 2.0 %fusion.48 = f32[2,512]{1,0:T(2,128)S(1)} fusion(f32[512,512]{0,1:T(8,128)S(1)} %subtract_convert_fusion, f32[2]{0:T(128)S(1)} %copy-done.4, pred[512,512]{0,1:T(8,128)(4,1)S(1)} %fusion.2, bf16[512,256]{1,0:T(8,128)(2,1)} %param.17, bf16[512,256]{1,0:T(8,128)(2,1)} %param.16), kind=kOutput, calls=%fused_computation.90 | convolution fusion | flops 137363968 | bytes 1839112 | tf_op jit(solution)/shard_map/sub | solution.py:30
  51.6 3.0 %convolution_convert_fusion = bf16[2,512,128]{1,2,0:T(8,128)(2,1)S(1)} fusion(bf16[512,2,128]{0,2,1:T(8,128)(2,1)} %bitcast.98, f32[2,512]{1,0:T(2,128)S(1)} %fusion.48, f32[2,512,512]{1,2,0:T(8,128)} %subtract_select_fusion), kind=kOutput, calls=%fused_computation.6 | convolution fusion | flops 135923200 | bytes 2625536 | tf_op jit(solution)/shard_map/hqk,khd->qhd/dot_general | solution.py:49
  54.6 0.9 constant_dynamic-slice_fusion.3
  58.9 0.9 constant_dynamic-slice_fusion.1
  65.0 75.5 %all-gather.2.cloned.1.call-done = bf16[514,2048]{0,1:T(8,128)(2,1)} async-done(((bf16[514,256]{0,1:T(8,128)(2,1)}), bf16[514,2048]{0,1:T(8,128)(2,1)}) %all-gather.2.cloned.1.call-update) | async-done | bytes 2105360 | tf_op jit(solution)/shard_map/all_gather | solution.py:135
  140.5 2.7 %fusion.53 = (f32[514]{0:T(1024)S(1)}, f32[514,256]{1,0:T(8,128)S(1)}) fusion(bf16[514,256]{1,0:T(8,128)(2,1)S(1)} %copy-done.8, f32[256]{0:T(256)S(1)} %copy-done.9, bf16[514,2048]{0,1:T(8,128)(2,1)} %all-gather.2.cloned.1.call-done, bf16[2048,256]{1,0:T(8,128)(2,1)S(1)} %copy-done), kind=kOutput, calls=%fused_computation.91 | convolution fusion | flops 539493888 | bytes 3946504 | tf_op jit(solution)/shard_map/dot_general | solution.py:134
  143.2 19.9 %psum.14 = f32[514]{0:T(1024)S(1)} all-reduce(f32[514]{0:T(1024)S(1)} %get-tuple-element.27), channel_id=1, replica_groups=mesh['rep'=64,'tp'=8] {'tp'}, use_global_device_ids=true, to_apply=%region_7.8 | all-reduce | flops 514 | bytes 4112 | tf_op jit(solution)/shard_map/psum | solution.py:142
  163.3 21.8 %psum.15 = f32[514]{0:T(1024)S(1)} all-reduce(f32[514]{0:T(1024)S(1)} %multiply_reduce_fusion), channel_id=1, replica_groups=mesh['rep'=64,'tp'=8] {'tp'}, use_global_device_ids=true, to_apply=%region_9.10 | all-reduce | flops 514 | bytes 4112 | tf_op jit(solution)/shard_map/psum | solution.py:144
  185.1 1.0 add_convert_fusion
  (75 shorter events, 13.4 us)
Async XLA Ops:
  7.2 133.3 %copy-start = (bf16[2048,256]{1,0:T(8,128)(2,1)S(1)}, bf16[2048,256]{1,0:T(8,128)(2,1)}, u32[]{:S(2)}) copy-start(bf16[2048,256]{1,0:T(8,128)(2,1)} %param.27) | copy-start | bytes 3145732
  7.2 21.1 %copy-start.3 = (bf16[2,256]{1,0:T(2,128)(2,1)S(1)}, bf16[2,256]{1,0:T(2,128)(2,1)}, u32[]{:S(2)}) copy-start(bf16[2,256]{1,0:T(2,128)(2,1)} %param.24) | copy-start | bytes 3076
  7.2 25.8 %copy-start.5 = (s32[128]{0:T(128)S(1)}, s32[128]{0:T(128)}, u32[]{:S(2)}) copy-start(s32[128]{0:T(128)} %param.25) | copy-start | bytes 1540
  7.2 133.3 %all-gather.2.cloned.1.call-start = ((), (), s32[]{:S(2)}) async-start(), calls=%async_computation | async-start | bytes 2949120 | tf_op jit(solution)/shard_map/all_gather | solution.py:135
  10.5 29.0 %copy-start.2 = (bf16[2,256]{1,0:T(2,128)(2,1)S(1)}, bf16[2,256]{1,0:T(2,128)(2,1)}, u32[]{:S(2)}) copy-start(bf16[2,256]{1,0:T(2,128)(2,1)} %param.22) | copy-start | bytes 3076
  11.6 42.9 %collective-permute-start.1 = (bf16[1024,256]{1,0:T(8,128)(2,1)S(1)}, bf16[1024,256]{1,0:T(8,128)(2,1)}, u32[]{:S(2)}, u32[]{:S(2)}) collective-permute-start(bf16[1024,256]{1,0:T(8,128)(2,1)S(1)} %dynamic-slice_bitcast_fusion.1), channel_id=1, source_target_pairs={{256,0},{264,8},{272,16},{280,24},{288,32},{296,40},{304,48},{312,... | collective-permute-start | bytes 1572872 | tf_op jit(solution)/shard_map/ppermute | solution.py:19
  17.7 38.7 %collective-permute-start.2 = (bf16[256]{0:T(256)(128)(2,1)}, bf16[256]{0:T(256)(128)(2,1)}, u32[]{:S(2)}, u32[]{:S(2)}) collective-permute-start(bf16[256]{0:T(256)(128)(2,1)} %get-tuple-element.10), channel_id=1, source_target_pairs={{256,0},{264,8},{272,16},{280,24},{288,32},{296,40},{304,48},{312,... | collective-permute-start | bytes 1544 | tf_op jit(solution)/shard_map/ppermute | solution.py:19
  21.4 35.8 %collective-permute-start = (bf16[256]{0:T(256)(128)(2,1)}, bf16[256]{0:T(256)(128)(2,1)}, u32[]{:S(2)}, u32[]{:S(2)}) collective-permute-start(bf16[256]{0:T(256)(128)(2,1)} %fusion.35), channel_id=1, source_target_pairs={{256,0},{264,8},{272,16},{280,24},{288,32},{296,40},{304,48},{312,... | collective-permute-start | bytes 1544 | tf_op jit(solution)/shard_map/ppermute | solution.py:19
  25.9 33.0 %collective-permute-start.3 = (bf16[1024,256]{1,0:T(8,128)(2,1)S(1)}, bf16[1024,256]{1,0:T(8,128)(2,1)}, u32[]{:S(2)}, u32[]{:S(2)}) collective-permute-start(bf16[1024,256]{1,0:T(8,128)(2,1)S(1)} %dynamic-slice_bitcast_fusion), channel_id=1, source_target_pairs={{256,0},{264,8},{272,16},{280,24},{288,32},{296,40},{304,48},{312,... | collective-permute-start | bytes 1572872 | tf_op jit(solution)/shard_map/ppermute | solution.py:19
  28.9 31.9 %collective-permute-start.4 = (bf16[256]{0:T(256)(128)(2,1)}, bf16[256]{0:T(256)(128)(2,1)}, u32[]{:S(2)}, u32[]{:S(2)}) collective-permute-start(bf16[256]{0:T(256)(128)(2,1)} %get-tuple-element.12), channel_id=1, source_target_pairs={{256,0},{264,8},{272,16},{280,24},{288,32},{296,40},{304,48},{312,... | collective-permute-start | bytes 1544 | tf_op jit(solution)/shard_map/ppermute | solution.py:19
  46.5 3.0 %copy-start.4 = (f32[2]{0:T(128)S(1)}, f32[2]{0:T(128)}, u32[]{:S(2)}) copy-start(f32[2]{0:T(128)} %multiply_exponential_fusion) | copy-start | bytes 28
  51.6 6.9 %copy-start.1 = (bf16[260,2,128]{2,1,0:T(2,128)(2,1)S(1)}, bf16[260,2,128]{2,1,0:T(2,128)(2,1)}, u32[]{:S(2)}) copy-start(bf16[260,2,128]{2,1,0:T(2,128)(2,1)} %pad_maximum_fusion.2) | copy-start | bytes 399364
  57.2 83.3 %copy-start.8 = (bf16[514,256]{1,0:T(8,128)(2,1)S(1)}, bf16[514,256]{1,0:T(8,128)(2,1)}, u32[]{:S(2)}) copy-start(bf16[514,256]{1,0:T(8,128)(2,1)} %param.29) | copy-start | bytes 789508
  57.2 83.3 %copy-start.9 = (f32[256]{0:T(256)S(1)}, f32[256]{0:T(256)}, u32[]{:S(2)}) copy-start(f32[256]{0:T(256)} %param.28) | copy-start | bytes 3076
  65.0 120.1 %copy-start.6 = (f32[256]{0:T(256)S(1)}, f32[256]{0:T(256)}, u32[]{:S(2)}) copy-start(f32[256]{0:T(256)} %param.31) | copy-start | bytes 3076
  65.0 120.1 %copy-start.7 = (f32[256]{0:T(256)S(1)}, f32[256]{0:T(256)}, u32[]{:S(2)}) copy-start(f32[256]{0:T(256)} %param.30) | copy-start | bytes 3076
Sparse Core Ops, SparseCore 0:
  62.9 77.5 all-gather.1
where the time goes:
time: 194 us; the launch traced here: 193 us
  waiting for transfers between devices  75.5 us (39%)
  blocking collectives  41.6 us (21%)
  between operations  21.3 us (11%)
  local copies, waits for them, and re-layouts  17.8 us (9%)
  starting transfers between devices  15.1 us (8%)
  matrix products  11.9 us (6%)
  other arithmetic  9.62 us (5%)
    all_gather x1, waiting for transfers between devices, on_device(): lax.all_gather(mixed_rows, 'tp', axis=1, tiled=True)  75.5 us
    psum x1, blocking collectives, on_device(): row_var = lax.psum(jnp.sum(centered * centered, axis=1), 'tp') / D  21.8 us
    psum x1, blocking collectives, on_device(): row_mean = lax.psum(row_total, 'tp') / D  19.9 us
    ppermute x5, starting transfers between devices, from_behind(): return lax.ppermute(block, axis, route)  15.1 us
  transfers between devices with their start and end apart: 6, of which 1 were waited for; matrix products, arithmetic and copies ran while one was open for 16% of the time, Pallas kernels for 0%

commit v1 on v0

--- a/solution.py
+++ b/solution.py
@@ -141,7 +141,7 @@
     row_total = jnp.sum(stream, axis=1)
     row_mean = lax.psum(row_total, "tp") / D
     centered = stream - row_mean[:, None]
-    row_var = lax.psum(jnp.sum(centered * centered, axis=1), "tp") / D
+    row_var = jnp.sum(lax.all_gather(jnp.sum(centered * centered, axis=1), "tp"), axis=0) / D
     normed = (
         centered * lax.rsqrt(row_var + norm_epsilon)[:, None] * ln_gain[None, :] + ln_shift[None, :]
     ).astype(jnp.bfloat16)

time: 194 us -> 212 us (1.093)
  blocking collectives: 41.6 us -> 59.2 us
    unnamed x0 -> x1, blocking collectives: none -> 39.4 us
    psum x1 -> x0, blocking collectives: 21.8 us -> none  [on_device(): row_var = lax.psum(jnp.sum(centered * centered, axis=1), 'tp') / D]
  transfers between devices with their start and end apart: 6 -> 6, of which waited for: 1 -> 1; matrix products, arithmetic and copies ran while one was open for 16% -> 15% of each run, Pallas kernels for 0% -> 0%
where the time goes in v1:
time: 212 us; the launch traced here: 211 us
  waiting for transfers between devices  73.6 us (35%)
  blocking collectives  59.2 us (28%)
  between operations  22 us (10%)
  local copies, waits for them, and re-layouts  19.5 us (9%)
  starting transfers between devices  15.1 us (7%)
  matrix products  11.9 us (6%)
  other arithmetic  9.63 us (5%)
    all_gather x1, waiting for transfers between devices, on_device(): lax.all_gather(mixed_rows, 'tp', axis=1, tiled=True)  73.6 us
    unnamed x1, blocking collectives  39.4 us
    psum x1, blocking collectives, on_device(): row_mean = lax.psum(row_total, 'tp') / D  19.9 us
    ppermute x5, starting transfers between devices, from_behind(): return lax.ppermute(block, axis, route)  15.1 us
  transfers between devices with their start and end apart: 6, of which 1 were waited for; matrix products, arithmetic and copies ran while one was open for 15% of the time, Pallas kernels for 0%

profile of v1, /device:TPU:32, one launch (start us, length us, event | category | flops | bytes accessed | tf_op | source)
XLA Modules:
  0.0 211.0 jit_solution(7276000116194837077)
XLA Ops:
  7.3 1.3 fusion.47
  10.6 1.1 dynamic-slice_bitcast_fusion.1
  11.6 3.4 %collective-permute-start.1 = (bf16[1024,256]{1,0:T(8,128)(2,1)S(1)}, bf16[1024,256]{1,0:T(8,128)(2,1)}, u32[]{:S(2)}, u32[]{:S(2)}) collective-permute-start(bf16[1024,256]{1,0:T(8,128)(2,1)S(1)} %dynamic-slice_bitcast_fusion.1), channel_id=1, source_target_pairs={{256,0},{264,8},{272,16},{280,24},{288,32},{296,40},{304,48},{312,... | collective-permute-start | bytes 1572872 | tf_op jit(solution)/shard_map/ppermute | solution.py:19
  16.3 1.4 fusion.33
  17.7 2.4 %collective-permute-start.2 = (bf16[256]{0:T(256)(128)(2,1)}, bf16[256]{0:T(256)(128)(2,1)}, u32[]{:S(2)}, u32[]{:S(2)}) collective-permute-start(bf16[256]{0:T(256)(128)(2,1)} %get-tuple-element.10), channel_id=1, source_target_pairs={{256,0},{264,8},{272,16},{280,24},{288,32},{296,40},{304,48},{312,... | collective-permute-start | bytes 1544 | tf_op jit(solution)/shard_map/ppermute | solution.py:19
  20.2 1.2 fusion.35
  21.4 3.4 %collective-permute-start = (bf16[256]{0:T(256)(128)(2,1)}, bf16[256]{0:T(256)(128)(2,1)}, u32[]{:S(2)}, u32[]{:S(2)}) collective-permute-start(bf16[256]{0:T(256)(128)(2,1)} %fusion.35), channel_id=1, source_target_pairs={{256,0},{264,8},{272,16},{280,24},{288,32},{296,40},{304,48},{312,... | collective-permute-start | bytes 1544 | tf_op jit(solution)/shard_map/ppermute | solution.py:19
  24.8 1.1 dynamic-slice_bitcast_fusion
  25.9 2.4 %collective-permute-start.3 = (bf16[1024,256]{1,0:T(8,128)(2,1)S(1)}, bf16[1024,256]{1,0:T(8,128)(2,1)}, u32[]{:S(2)}, u32[]{:S(2)}) collective-permute-start(bf16[1024,256]{1,0:T(8,128)(2,1)S(1)} %dynamic-slice_bitcast_fusion), channel_id=1, source_target_pairs={{256,0},{264,8},{272,16},{280,24},{288,32},{296,40},{304,48},{312,... | collective-permute-start | bytes 1572872 | tf_op jit(solution)/shard_map/ppermute | solution.py:19
  28.9 3.4 %collective-permute-start.4 = (bf16[256]{0:T(256)(128)(2,1)}, bf16[256]{0:T(256)(128)(2,1)}, u32[]{:S(2)}, u32[]{:S(2)}) collective-permute-start(bf16[256]{0:T(256)(128)(2,1)} %get-tuple-element.12), channel_id=1, source_target_pairs={{256,0},{264,8},{272,16},{280,24},{288,32},{296,40},{304,48},{312,... | collective-permute-start | bytes 1544 | tf_op jit(solution)/shard_map/ppermute | solution.py:19
  38.1 1.0 constant_dynamic-slice_fusion.6
  41.2 1.8 copy.50
  43.0 2.0 fusion.24
  45.0 1.5 pad_maximum_fusion.2
  46.5 3.0 %subtract_select_fusion = f32[2,512,512]{1,2,0:T(8,128)} fusion(f32[512,512]{0,1:T(8,128)S(1)} %subtract_convert_fusion, f32[2]{0:T(128)} %multiply_exponential_fusion, pred[512,512]{0,1:T(8,128)(4,1)S(1)} %fusion.2, bf16[512,256]{1,0:T(8,128)(2,1)} %param.17, bf16[512,256]{1,0:T(8,128)(2,1)} %param.16), kind=kOutput, calls=%fused_computation.3 | convolution fusion | flops 136314880 | bytes 3932168 | tf_op jit(solution)/shard_map/qhd,khd->hqk/dot_general | solution.py:40
  49.5 2.0 fusion.48
  51.6 3.0 %convolution_convert_fusion = bf16[2,512,128]{1,2,0:T(8,128)(2,1)S(1)} fusion(bf16[512,2,128]{0,2,1:T(8,128)(2,1)} %bitcast.99, f32[2,512]{1,0:T(2,128)S(1)} %fusion.48, f32[2,512,512]{1,2,0:T(8,128)} %subtract_select_fusion), kind=kOutput, calls=%fused_computation.6 | convolution fusion | flops 135923200 | bytes 2625536 | tf_op jit(solution)/shard_map/hqk,khd->qhd/dot_general | solution.py:49
  54.6 0.9 constant_dynamic-slice_fusion.3
  62.8 1.3 dynamic-slice.4
  66.9 73.6 %all-gather.3.cloned.1.call-done = bf16[514,2048]{0,1:T(8,128)(2,1)} async-done(((bf16[514,256]{0,1:T(8,128)(2,1)}), bf16[514,2048]{0,1:T(8,128)(2,1)}) %all-gather.3.cloned.1.call-update) | async-done | bytes 2105360 | tf_op jit(solution)/shard_map/all_gather | solution.py:135
  140.5 2.7 %fusion.53 = (f32[514]{0:T(1024)S(1)}, f32[514,256]{1,0:T(8,128)S(1)}) fusion(bf16[514,256]{1,0:T(8,128)(2,1)S(1)} %copy-done.8, f32[256]{0:T(256)S(1)} %copy-done.9, bf16[514,2048]{0,1:T(8,128)(2,1)} %all-gather.3.cloned.1.call-done, bf16[2048,256]{1,0:T(8,128)(2,1)S(1)} %copy-done), kind=kOutput, calls=%fused_computation.91 | convolution fusion | flops 539493888 | bytes 3946504 | tf_op jit(solution)/shard_map/dot_general | solution.py:134
  143.2 19.9 %psum.7 = f32[514]{0:T(1024)S(1)} all-reduce(f32[514]{0:T(1024)S(1)} %get-tuple-element.27), channel_id=1, replica_groups=mesh['rep'=64,'tp'=8] {'tp'}, use_global_device_ids=true, to_apply=%region_7.8 | all-reduce | flops 514 | bytes 4112 | tf_op jit(solution)/shard_map/psum | solution.py:142
  163.7 39.4 %all-reduce = f32[4112]{0:T(1024)S(1)} all-reduce(f32[4112]{0:T(1024)S(1)} %dynamic-update-slice), channel_id=2, replica_groups=mesh['rep'=64,'tp'=8] {'tp'}, use_global_device_ids=true, to_apply=%add | all-reduce | flops 4112 | bytes 32896
  203.2 1.0 add_convert_fusion
  (80 shorter events, 14.7 us)
Async XLA Ops:
  7.2 133.3 %copy-start = (bf16[2048,256]{1,0:T(8,128)(2,1)S(1)}, bf16[2048,256]{1,0:T(8,128)(2,1)}, u32[]{:S(2)}) copy-start(bf16[2048,256]{1,0:T(8,128)(2,1)} %param.27) | copy-start | bytes 3145732
  7.2 21.1 %copy-start.3 = (bf16[2,256]{1,0:T(2,128)(2,1)S(1)}, bf16[2,256]{1,0:T(2,128)(2,1)}, u32[]{:S(2)}) copy-start(bf16[2,256]{1,0:T(2,128)(2,1)} %param.24) | copy-start | bytes 3076
  7.2 25.8 %copy-start.5 = (s32[128]{0:T(128)S(1)}, s32[128]{0:T(128)}, u32[]{:S(2)}) copy-start(s32[128]{0:T(128)} %param.25) | copy-start | bytes 1540
  7.2 133.3 %all-gather.3.cloned.1.call-start = ((), (), s32[]{:S(2)}) async-start(), calls=%async_computation | async-start | bytes 2949120 | tf_op jit(solution)/shard_map/all_gather | solution.py:135
  10.5 29.0 %copy-start.2 = (bf16[2,256]{1,0:T(2,128)(2,1)S(1)}, bf16[2,256]{1,0:T(2,128)(2,1)}, u32[]{:S(2)}) copy-start(bf16[2,256]{1,0:T(2,128)(2,1)} %param.22) | copy-start | bytes 3076
  11.6 42.9 %collective-permute-start.1 = (bf16[1024,256]{1,0:T(8,128)(2,1)S(1)}, bf16[1024,256]{1,0:T(8,128)(2,1)}, u32[]{:S(2)}, u32[]{:S(2)}) collective-permute-start(bf16[1024,256]{1,0:T(8,128)(2,1)S(1)} %dynamic-slice_bitcast_fusion.1), channel_id=1, source_target_pairs={{256,0},{264,8},{272,16},{280,24},{288,32},{296,40},{304,48},{312,... | collective-permute-start | bytes 1572872 | tf_op jit(solution)/shard_map/ppermute | solution.py:19
  17.7 38.7 %collective-permute-start.2 = (bf16[256]{0:T(256)(128)(2,1)}, bf16[256]{0:T(256)(128)(2,1)}, u32[]{:S(2)}, u32[]{:S(2)}) collective-permute-start(bf16[256]{0:T(256)(128)(2,1)} %get-tuple-element.10), channel_id=1, source_target_pairs={{256,0},{264,8},{272,16},{280,24},{288,32},{296,40},{304,48},{312,... | collective-permute-start | bytes 1544 | tf_op jit(solution)/shard_map/ppermute | solution.py:19
  21.4 35.8 %collective-permute-start = (bf16[256]{0:T(256)(128)(2,1)}, bf16[256]{0:T(256)(128)(2,1)}, u32[]{:S(2)}, u32[]{:S(2)}) collective-permute-start(bf16[256]{0:T(256)(128)(2,1)} %fusion.35), channel_id=1, source_target_pairs={{256,0},{264,8},{272,16},{280,24},{288,32},{296,40},{304,48},{312,... | collective-permute-start | bytes 1544 | tf_op jit(solution)/shard_map/ppermute | solution.py:19
  25.9 33.0 %collective-permute-start.3 = (bf16[1024,256]{1,0:T(8,128)(2,1)S(1)}, bf16[1024,256]{1,0:T(8,128)(2,1)}, u32[]{:S(2)}, u32[]{:S(2)}) collective-permute-start(bf16[1024,256]{1,0:T(8,128)(2,1)S(1)} %dynamic-slice_bitcast_fusion), channel_id=1, source_target_pairs={{256,0},{264,8},{272,16},{280,24},{288,32},{296,40},{304,48},{312,... | collective-permute-start | bytes 1572872 | tf_op jit(solution)/shard_map/ppermute | solution.py:19
  28.9 31.9 %collective-permute-start.4 = (bf16[256]{0:T(256)(128)(2,1)}, bf16[256]{0:T(256)(128)(2,1)}, u32[]{:S(2)}, u32[]{:S(2)}) collective-permute-start(bf16[256]{0:T(256)(128)(2,1)} %get-tuple-element.12), channel_id=1, source_target_pairs={{256,0},{264,8},{272,16},{280,24},{288,32},{296,40},{304,48},{312,... | collective-permute-start | bytes 1544 | tf_op jit(solution)/shard_map/ppermute | solution.py:19
  46.5 3.0 %copy-start.4 = (f32[2]{0:T(128)S(1)}, f32[2]{0:T(128)}, u32[]{:S(2)}) copy-start(f32[2]{0:T(128)} %multiply_exponential_fusion) | copy-start | bytes 28
  51.6 6.9 %copy-start.1 = (bf16[260,2,128]{2,1,0:T(2,128)(2,1)S(1)}, bf16[260,2,128]{2,1,0:T(2,128)(2,1)}, u32[]{:S(2)}) copy-start(bf16[260,2,128]{2,1,0:T(2,128)(2,1)} %pad_maximum_fusion.2) | copy-start | bytes 399364
  57.2 83.3 %copy-start.8 = (bf16[514,256]{1,0:T(8,128)(2,1)S(1)}, bf16[514,256]{1,0:T(8,128)(2,1)}, u32[]{:S(2)}) copy-start(bf16[514,256]{1,0:T(8,128)(2,1)} %param.29) | copy-start | bytes 789508
  57.2 83.3 %copy-start.9 = (f32[256]{0:T(256)S(1)}, f32[256]{0:T(256)}, u32[]{:S(2)}) copy-start(f32[256]{0:T(256)} %param.28) | copy-start | bytes 3076
  66.9 136.2 %copy-start.6 = (f32[256]{0:T(256)S(1)}, f32[256]{0:T(256)}, u32[]{:S(2)}) copy-start(f32[256]{0:T(256)} %param.31) | copy-start | bytes 3076
  66.9 136.3 %copy-start.7 = (f32[256]{0:T(256)S(1)}, f32[256]{0:T(256)}, u32[]{:S(2)}) copy-start(f32[256]{0:T(256)} %param.30) | copy-start | bytes 3076
Sparse Core Ops, SparseCore 0:
  62.9 77.5 all-gather.2
